TPU v7x, 128 devices: a whole 4x4x4 slice. The times are simulated.
128 devices in a mesh: smp: 8 (over y, core), gx: 8 (over z_lo, x), gz: 2 (over z_hi).
Axes of the slice: x: 4, y: 4, z: 4 (z_hi: 2, z_lo: 2; z = z_hi * 2 + z_lo), core: 2. Of those that a mesh axis runs over, the one named last changes fastest.
Arguments:
- features: bfloat16 [8, 32, 40, 8, 256], P('smp', None, 'gx', None, 'gz'), may hold values from -6 to 6
- first_weight: bfloat16 [32, 3, 3, 3, 32], replicated, may hold values from -0.21875 to 0.21875
- first_bias: float32 [32], replicated, may hold values from -1 to 1
- second_weight: bfloat16 [32, 3, 3, 3, 32], replicated, may hold values from -0.21875 to 0.21875
- second_bias: float32 [32], replicated, may hold values from -1 to 1
- cotangent: bfloat16 [8, 32, 40, 8, 256], P('smp', None, 'gx', None, 'gz'), may hold values from -6 to 6
Outputs:
- output: bfloat16 [8, 32, 40, 8, 256], P('smp', None, 'gx', None, 'gz')
- first_grad: float32 [32, 3, 3, 3, 32], replicated
- first_bias_grad: float32 [32], replicated
- second_grad: float32 [32, 3, 3, 3, 32], replicated
- second_bias_grad: float32 [32], replicated
All inputs are finite; a program needn't handle non-finite values.
Results may differ from a plain program's by a relative error of at most 0.011.
Values may be sent and summed in bfloat16 or wider, within the bound.
A program may use at most 128 MiB of HBM per device.

v0:
```python
import jax
import jax.numpy as jnp
from jax import lax
from jax.sharding import PartitionSpec as P


def extended(array, sides, width):
    for axis, dim in sides:
        size, length = (lax.axis_size(axis), array.shape[dim])
        up = [(i, (i + 1) % size) for i in range(size)]
        down = [(j, i) for i, j in up]
        last = lax.slice_in_dim(array, length - width, length, axis=dim)
        initial = lax.slice_in_dim(array, 0, width, axis=dim)
        before = lax.ppermute(last, axis, up)
        after = lax.ppermute(initial, axis, down)
        array = jnp.concatenate([before, array, after], axis=dim)
    return array


def wall_pad(field_in):
    return jnp.pad(field_in, ((0, 0), (0, 0), (0, 0), (1, 1), (0, 0)))


def extend(field_in, depth_cells):
    both_wide = extended(field_in, (("gx", 2), ("gz", 4)), depth_cells)
    return wall_pad(both_wide)


def stack_taps(padded, offset_x, offset_y, cells_x, cells_y, cells_z):
    return jnp.concatenate(
        [
            padded[
                :,
                :,
                offset_x : offset_x + cells_x,
                offset_y : offset_y + cells_y,
                offset_z : offset_z + cells_z,
            ]
            for offset_z in range(3)
        ],
        axis=1,
    )


def convolve(padded, weight):
    cells_x = padded.shape[2] - 2
    cells_y = padded.shape[3] - 2
    cells_z = padded.shape[4] - 2
    summed = jnp.zeros((padded.shape[0], weight.shape[0], cells_x, cells_y, cells_z), jnp.float32)
    for offset_x in range(3):
        for offset_y in range(3):
            stacked = stack_taps(padded, offset_x, offset_y, cells_x, cells_y, cells_z)
            tap_block = weight[:, offset_x, offset_y].reshape(weight.shape[0], -1)
            summed = summed + jnp.einsum(
                "ok,skxyz->soxyz", tap_block, stacked, preferred_element_type=jnp.float32
            )
    return summed


def correlate(upstream, padded):
    cells_x = upstream.shape[2]
    cells_y = upstream.shape[3]
    cells_z = upstream.shape[4]
    outer_terms = []
    for offset_x in range(3):
        inner_terms = []
        for offset_y in range(3):
            stacked = stack_taps(padded, offset_x, offset_y, cells_x, cells_y, cells_z)
            local_term = jnp.einsum(
                "soxyz,skxyz->ok", upstream, stacked, preferred_element_type=jnp.float32
            )
            inner_terms.append(local_term.reshape(upstream.shape[1], 3, -1))
        outer_terms.append(jnp.stack(inner_terms, axis=1))
    return jnp.stack(outer_terms, axis=1)


def shards(features, first_weight, first_bias, second_weight, second_bias, cotangent):
    input_pad = extend(features, 1)
    preact = convolve(input_pad, first_weight) + first_bias[None, :, None, None, None]
    hidden = jax.nn.silu(preact).astype(jnp.bfloat16)
    hidden_pad = extend(hidden, 1)
    residual_term = convolve(hidden_pad, second_weight) + second_bias[None, :, None, None, None]
    output = (features.astype(jnp.float32) + residual_term).astype(jnp.bfloat16)
    cells_all = (
        features.shape[0]
        * lax.axis_size("smp")
        * features.shape[2]
        * lax.axis_size("gx")
        * features.shape[3]
        * features.shape[4]
        * lax.axis_size("gz")
    )
    grad_scale = 1.0 / cells_all**0.5
    second_grad = correlate(cotangent, hidden_pad) * grad_scale
    second_bgrad = jnp.sum(cotangent, axis=(0, 2, 3, 4), dtype=jnp.float32) * grad_scale
    flipped = jnp.transpose(jnp.flip(second_weight, (1, 2, 3)), (4, 1, 2, 3, 0))
    upstream_pad = extend(cotangent, 1)
    hidden_grad = convolve(upstream_pad, flipped)
    logistic = jax.nn.sigmoid(preact)
    preact_grad = (hidden_grad * logistic * (1.0 + preact * (1.0 - logistic))).astype(jnp.bfloat16)
    first_grad = correlate(preact_grad, input_pad) * grad_scale
    first_bgrad = jnp.sum(preact_grad, axis=(0, 2, 3, 4), dtype=jnp.float32) * grad_scale
    first_grad, first_bgrad, second_grad, second_bgrad = lax.psum(
        (first_grad, first_bgrad, second_grad, second_bgrad), ("smp", "gx", "gz")
    )
    return (output, first_grad, first_bgrad, second_grad, second_bgrad)


def solution(mesh):
    in_specs = (
        P("smp", None, "gx", None, "gz"),
        P(),
        P(),
        P(),
        P(),
        P("smp", None, "gx", None, "gz"),
    )
    out_specs = (P("smp", None, "gx", None, "gz"), P(), P(), P(), P())
    return jax.shard_map(shards, mesh=mesh, in_specs=in_specs, out_specs=out_specs, check_vma=False)
```

profile of v0, /device:TPU:1, one launch (start us, length us, event | category | flops | bytes accessed | tf_op | source)
XLA Modules:
  0.0 336.7 jit_solution(1771370892015134245)
XLA Ops:
  7.2 1.1 copy.113
  8.3 4.7 %collective-permute-start.9 = (bf16[1,32,1,8,128]{4,1,3,2,0:T(8,128)(2,1)S(1)}, bf16[1,32,1,8,128]{4,1,3,2,0:T(8,128)(2,1)S(1)}, u32[]{:S(2)}, u32[]{:S(2)}) collective-permute-start(bf16[1,32,1,8,128]{4,1,3,2,0:T(8,128)(2,1)S(1)} %get-tuple-element.105), channel_id=1, source_target_pairs={{2,0},{4,2},{6,4},{8,6},{10,8},{12,10},{14,12},{0,14},{3,1},{5,3},... | collective-permute-start | bytes 196616 | tf_op jit(solution)/shard_map/ppermute | solution.py:15
  13.1 1.1 copy.88
  14.2 3.6 %collective-permute-start.1 = (bf16[1,32,1,8,128]{4,1,3,2,0:T(8,128)(2,1)S(1)}, bf16[1,32,1,8,128]{4,1,3,2,0:T(8,128)(2,1)S(1)}, u32[]{:S(2)}, u32[]{:S(2)}) collective-permute-start(bf16[1,32,1,8,128]{4,1,3,2,0:T(8,128)(2,1)S(1)} %get-tuple-element.109), channel_id=1, source_target_pairs={{2,0},{4,2},{6,4},{8,6},{10,8},{12,10},{14,12},{0,14},{3,1},{5,3},... | collective-permute-start | bytes 196616 | tf_op jit(solution)/shard_map/ppermute | solution.py:15
  20.6 2.4 collective-permute-done
  23.1 3.4 %collective-permute-start.10 = (bf16[1,32,7,8,1]{4,1,3,2,0:T(8,128)(2,1)S(1)}, bf16[1,32,7,8,1]{4,1,3,2,0:T(8,128)(2,1)S(1)}, u32[]{:S(2)}, u32[]{:S(2)}) collective-permute-start(bf16[1,32,7,8,1]{4,1,3,2,0:T(8,128)(2,1)S(1)} %get-tuple-element.89), channel_id=1, source_target_pairs={{0,1},{1,0},{2,3},{3,2},{4,5},{5,4},{6,7},{7,6},{8,9},{9,8},{10,11... | collective-permute-start | bytes 10760 | tf_op jit(solution)/shard_map/ppermute | solution.py:14
  26.8 3.0 collective-permute-start.2
  29.8 4.7 %collective-permute-done.10 = bf16[1,32,7,8,1]{4,1,3,2,0:T(8,128)(2,1)S(1)} collective-permute-done((bf16[1,32,7,8,1]{4,1,3,2,0:T(8,128)(2,1)S(1)}, bf16[1,32,7,8,1]{4,1,3,2,0:T(8,128)(2,1)S(1)}, u32[]{:S(2)}, u32[]{:S(2)}) %collective-permute-start.10) | collective-permute-done | bytes 3616 | tf_op jit(solution)/shard_map/ppermute | solution.py:14
  34.5 9.8 %collective-permute-done.11 = bf16[1,32,7,8,1]{4,1,3,2,0:T(8,128)(2,1)S(1)} collective-permute-done((bf16[1,32,7,8,1]{4,1,3,2,0:T(8,128)(2,1)S(1)}, bf16[1,32,7,8,1]{4,1,3,2,0:T(8,128)(2,1)S(1)}, u32[]{:S(2)}, u32[]{:S(2)}) %collective-permute-start.11) | collective-permute-done | bytes 3616 | tf_op jit(solution)/shard_map/ppermute | solution.py:15
  44.9 1.5 fusion.148
  46.5 7.7 %collective-permute-done.2 = bf16[1,32,7,8,1]{4,1,3,2,0:T(8,128)(2,1)S(1)} collective-permute-done((bf16[1,32,7,8,1]{4,1,3,2,0:T(8,128)(2,1)S(1)}, bf16[1,32,7,8,1]{4,1,3,2,0:T(8,128)(2,1)S(1)}, u32[]{:S(2)}, u32[]{:S(2)}) %collective-permute-start.2) | collective-permute-done | bytes 3616 | tf_op jit(solution)/shard_map/ppermute | solution.py:14
  54.2 9.8 %collective-permute-done.3 = bf16[1,32,7,8,1]{4,1,3,2,0:T(8,128)(2,1)S(1)} collective-permute-done((bf16[1,32,7,8,1]{4,1,3,2,0:T(8,128)(2,1)S(1)}, bf16[1,32,7,8,1]{4,1,3,2,0:T(8,128)(2,1)S(1)}, u32[]{:S(2)}, u32[]{:S(2)}) %collective-permute-start.3) | collective-permute-done | bytes 3616 | tf_op jit(solution)/shard_map/ppermute | solution.py:15
  64.6 1.5 fusion.150
  67.1 1.1 pad_maximum_fusion.14
  74.2 1.0 convolution_add_fusion.1
  76.6 0.7 convolution_bitcast_fusion.5
  78.7 0.7 convolution_bitcast_fusion.1
  79.4 0.7 convolution_bitcast_fusion.7
  81.6 0.7 convolution_bitcast_fusion
  82.4 3.6 %collective-permute-start.5 = (bf16[1,32,1,8,128]{4,1,3,2,0:T(8,128)(2,1)S(1)}, bf16[1,32,1,8,128]{4,1,3,2,0:T(8,128)(2,1)S(1)}, u32[]{:S(2)}, u32[]{:S(2)}) collective-permute-start(bf16[1,32,1,8,128]{4,1,3,2,0:T(8,128)(2,1)S(1)} %get-tuple-element.108), channel_id=1, source_target_pairs={{2,0},{4,2},{6,4},{8,6},{10,8},{12,10},{14,12},{0,14},{3,1},{5,3},... | collective-permute-start | bytes 196616 | tf_op jit(solution)/shard_map/ppermute | solution.py:15
  86.0 1.6 collective-permute-done.4
  87.9 2.8 collective-permute-start.6
  91.0 0.8 maximum_multiply_fusion
  91.8 78.4 %all-reduce.3 = (f32[32]{0:T(128)}, f32[32]{0:T(128)}) all-reduce(f32[32]{0:T(128)S(1)} %broadcast_multiply_fusion.1, f32[32]{0:T(128)S(1)} %broadcast_multiply_fusion), channel_id=1, replica_groups=mesh['smp'=8,'gx'=8,'gz'=2] {'smp','gx','gz'}, use_global_device_ids=true, to_apply=%region_2.3 | all-reduce | flops 64 | bytes 512 | tf_op jit(solution)/shard_map/psum | solution.py:103
  174.4 1.4 fusion.149
  176.7 0.7 convolution_bitcast_fusion.9
  180.3 0.7 convolution_bitcast_fusion.15
  183.0 0.8 maximum_multiply_fusion.1
  184.1 0.9 copy.164
  185.0 142.2 %all-reduce.7.cloned.1.call-done = (f32[32,3,3,3,32]{4,0,3,2,1:T(8,128)}, f32[32,3,3,3,32]{4,0,3,2,1:T(8,128)}) async-done(((f32[32,3,3,3,32]{4,0,3,2,1:T(8,128)}, f32[32,3,3,3,32]{4,0,3,2,1:T(8,128)}), (f32[32,3,3,3,32]{4,0,3,2,1:T(8,128)}, f32[32,3,3,3,32]{4,0,3,2,1:T(8,128)})) %all-reduce.7.cloned.1.call-update) | async-done | bytes 221200 | tf_op jit(solution)/shard_map/psum | solution.py:103
  327.2 1.9 copy.328
  329.1 0.8 copy.329
  (142 shorter events, 26.3 us)
Async XLA Ops:
  7.2 10.6 %copy-start = (bf16[1,32,5,8,128]{4,3,2,1,0:T(8,128)(2,1)S(1)}, bf16[1,32,5,8,128]{4,3,2,1,0:T(8,128)(2,1)}, u32[]{:S(2)}) copy-start(bf16[1,32,5,8,128]{4,3,2,1,0:T(8,128)(2,1)} %param.11) | copy-start | bytes 983044
  7.2 10.9 %copy-start.2 = (bf16[32,3,3,3,32]{4,0,3,2,1:T(8,128)(2,1)S(1)}, bf16[32,3,3,3,32]{4,0,3,2,1:T(8,128)(2,1)}, u32[]{:S(2)}) copy-start(bf16[32,3,3,3,32]{4,0,3,2,1:T(8,128)(2,1)} %param.9) | copy-start | bytes 165892
  7.2 320.0 %all-reduce.7.cloned.1.call-start = ((), (), s32[]{:S(2)}) async-start(), calls=%async_computation | async-start | bytes 1769472 | tf_op jit(solution)/shard_map/psum | solution.py:103
  8.3 12.0 %collective-permute-start.9 = (bf16[1,32,1,8,128]{4,1,3,2,0:T(8,128)(2,1)S(1)}, bf16[1,32,1,8,128]{4,1,3,2,0:T(8,128)(2,1)S(1)}, u32[]{:S(2)}, u32[]{:S(2)}) collective-permute-start(bf16[1,32,1,8,128]{4,1,3,2,0:T(8,128)(2,1)S(1)} %get-tuple-element.105), channel_id=1, source_target_pairs={{2,0},{4,2},{6,4},{8,6},{10,8},{12,10},{14,12},{0,14},{3,1},{5,3},... | collective-permute-start | bytes 196616 | tf_op jit(solution)/shard_map/ppermute | solution.py:15
  13.1 5.1 %copy-start.4 = (bf16[32,3,3,3,32]{4,0,3,2,1:T(8,128)(2,1)S(1)}, bf16[32,3,3,3,32]{4,0,3,2,1:T(8,128)(2,1)}, u32[]{:S(2)}) copy-start(bf16[32,3,3,3,32]{4,0,3,2,1:T(8,128)(2,1)} %param.7) | copy-start | bytes 165892
  13.1 7.2 %collective-permute-start.8 = (bf16[1,32,1,8,128]{4,1,3,2,0:T(8,128)(2,1)S(1)}, bf16[1,32,1,8,128]{4,1,3,2,0:T(8,128)(2,1)S(1)}, u32[]{:S(2)}, u32[]{:S(2)}) collective-permute-start(bf16[1,32,1,8,128]{4,1,3,2,0:T(8,128)(2,1)S(1)} %get-tuple-element.106), channel_id=1, source_target_pairs={{0,2},{2,4},{4,6},{6,8},{8,10},{10,12},{12,14},{14,0},{1,3},{3,5},... | collective-permute-start | bytes 196616 | tf_op jit(solution)/shard_map/ppermute | solution.py:14
  14.2 12.4 %collective-permute-start.1 = (bf16[1,32,1,8,128]{4,1,3,2,0:T(8,128)(2,1)S(1)}, bf16[1,32,1,8,128]{4,1,3,2,0:T(8,128)(2,1)S(1)}, u32[]{:S(2)}, u32[]{:S(2)}) collective-permute-start(bf16[1,32,1,8,128]{4,1,3,2,0:T(8,128)(2,1)S(1)} %get-tuple-element.109), channel_id=1, source_target_pairs={{2,0},{4,2},{6,4},{8,6},{10,8},{12,10},{14,12},{0,14},{3,1},{5,3},... | collective-permute-start | bytes 196616 | tf_op jit(solution)/shard_map/ppermute | solution.py:15
  17.8 5.2 %collective-permute-start = (bf16[1,32,1,8,128]{4,1,3,2,0:T(8,128)(2,1)S(1)}, bf16[1,32,1,8,128]{4,1,3,2,0:T(8,128)(2,1)S(1)}, u32[]{:S(2)}, u32[]{:S(2)}) collective-permute-start(bf16[1,32,1,8,128]{4,1,3,2,0:T(8,128)(2,1)S(1)} %get-tuple-element.110), channel_id=1, source_target_pairs={{0,2},{2,4},{4,6},{6,8},{8,10},{10,12},{12,14},{14,0},{1,3},{3,5},... | collective-permute-start | bytes 196616 | tf_op jit(solution)/shard_map/ppermute | solution.py:14
  20.3 2.7 copy-start.1
  23.1 11.4 %collective-permute-start.10 = (bf16[1,32,7,8,1]{4,1,3,2,0:T(8,128)(2,1)S(1)}, bf16[1,32,7,8,1]{4,1,3,2,0:T(8,128)(2,1)S(1)}, u32[]{:S(2)}, u32[]{:S(2)}) collective-permute-start(bf16[1,32,7,8,1]{4,1,3,2,0:T(8,128)(2,1)S(1)} %get-tuple-element.89), channel_id=1, source_target_pairs={{0,1},{1,0},{2,3},{3,2},{4,5},{5,4},{6,7},{7,6},{8,9},{9,8},{10,11... | collective-permute-start | bytes 10760 | tf_op jit(solution)/shard_map/ppermute | solution.py:14
  26.5 17.9 %collective-permute-start.11 = (bf16[1,32,7,8,1]{4,1,3,2,0:T(8,128)(2,1)S(1)}, bf16[1,32,7,8,1]{4,1,3,2,0:T(8,128)(2,1)S(1)}, u32[]{:S(2)}, u32[]{:S(2)}) collective-permute-start(bf16[1,32,7,8,1]{4,1,3,2,0:T(8,128)(2,1)S(1)} %get-tuple-element.90), channel_id=1, source_target_pairs={{1,0},{0,1},{3,2},{2,3},{5,4},{4,5},{7,6},{6,7},{9,8},{8,9},{11,10... | collective-permute-start | bytes 10760 | tf_op jit(solution)/shard_map/ppermute | solution.py:15
  26.8 27.4 %collective-permute-start.2 = (bf16[1,32,7,8,1]{4,1,3,2,0:T(8,128)(2,1)S(1)}, bf16[1,32,7,8,1]{4,1,3,2,0:T(8,128)(2,1)S(1)}, u32[]{:S(2)}, u32[]{:S(2)}) collective-permute-start(bf16[1,32,7,8,1]{4,1,3,2,0:T(8,128)(2,1)S(1)} %get-tuple-element.97), channel_id=1, source_target_pairs={{0,1},{1,0},{2,3},{3,2},{4,5},{5,4},{6,7},{7,6},{8,9},{9,8},{10,11... | collective-permute-start | bytes 10760 | tf_op jit(solution)/shard_map/ppermute | solution.py:14
  29.8 34.3 %collective-permute-start.3 = (bf16[1,32,7,8,1]{4,1,3,2,0:T(8,128)(2,1)S(1)}, bf16[1,32,7,8,1]{4,1,3,2,0:T(8,128)(2,1)S(1)}, u32[]{:S(2)}, u32[]{:S(2)}) collective-permute-start(bf16[1,32,7,8,1]{4,1,3,2,0:T(8,128)(2,1)S(1)} %get-tuple-element.98), channel_id=1, source_target_pairs={{1,0},{0,1},{3,2},{2,3},{5,4},{4,5},{7,6},{6,7},{9,8},{8,9},{11,10... | collective-permute-start | bytes 10760 | tf_op jit(solution)/shard_map/ppermute | solution.py:15
  70.4 0.7 copy-start.5
  82.3 5.3 %collective-permute-start.4 = (bf16[1,32,1,8,128]{4,1,3,2,0:T(8,128)(2,1)S(1)}, bf16[1,32,1,8,128]{4,1,3,2,0:T(8,128)(2,1)S(1)}, u32[]{:S(2)}, u32[]{:S(2)}) collective-permute-start(bf16[1,32,1,8,128]{4,1,3,2,0:T(8,128)(2,1)S(1)} %get-tuple-element.107), channel_id=1, source_target_pairs={{0,2},{2,4},{4,6},{6,8},{8,10},{10,12},{12,14},{14,0},{1,3},{3,5},... | collective-permute-start | bytes 196616 | tf_op jit(solution)/shard_map/ppermute | solution.py:14
  82.4 5.2 %collective-permute-start.5 = (bf16[1,32,1,8,128]{4,1,3,2,0:T(8,128)(2,1)S(1)}, bf16[1,32,1,8,128]{4,1,3,2,0:T(8,128)(2,1)S(1)}, u32[]{:S(2)}, u32[]{:S(2)}) collective-permute-start(bf16[1,32,1,8,128]{4,1,3,2,0:T(8,128)(2,1)S(1)} %get-tuple-element.108), channel_id=1, source_target_pairs={{2,0},{4,2},{6,4},{8,6},{10,8},{12,10},{14,12},{0,14},{3,1},{5,3},... | collective-permute-start | bytes 196616 | tf_op jit(solution)/shard_map/ppermute | solution.py:15
  87.9 82.2 %collective-permute-start.6 = (bf16[1,32,7,8,1]{4,1,3,2,0:T(8,128)(2,1)S(1)}, bf16[1,32,7,8,1]{4,1,3,2,0:T(8,128)(2,1)S(1)}, u32[]{:S(2)}, u32[]{:S(2)}) collective-permute-start(bf16[1,32,7,8,1]{4,1,3,2,0:T(8,128)(2,1)S(1)} %get-tuple-element.93), channel_id=1, source_target_pairs={{0,1},{1,0},{2,3},{3,2},{4,5},{5,4},{6,7},{7,6},{8,9},{9,8},{10,11... | collective-permute-start | bytes 10760 | tf_op jit(solution)/shard_map/ppermute | solution.py:14
  90.7 79.5 %collective-permute-start.7 = (bf16[1,32,7,8,1]{4,1,3,2,0:T(8,128)(2,1)S(1)}, bf16[1,32,7,8,1]{4,1,3,2,0:T(8,128)(2,1)S(1)}, u32[]{:S(2)}, u32[]{:S(2)}) collective-permute-start(bf16[1,32,7,8,1]{4,1,3,2,0:T(8,128)(2,1)S(1)} %get-tuple-element.94), channel_id=1, source_target_pairs={{1,0},{0,1},{3,2},{2,3},{5,4},{4,5},{7,6},{6,7},{9,8},{8,9},{11,10... | collective-permute-start | bytes 10760 | tf_op jit(solution)/shard_map/ppermute | solution.py:15
  182.9 0.9 copy-start.6
  327.2 1.9 copy-start.3
Sparse Core Ops, SparseCore 0:
  184.0 143.2 all-reduce.6
where the time goes:
time: 337 us
  waiting for transfers between devices  178 us (53%)
  blocking collectives  78.4 us (23%)
  starting transfers between devices  21.6 us (6%)
  matrix products  21.5 us (6%)
  between operations  14.6 us (4%)
  local copies, waits for them, and re-layouts  14 us (4%)
  other arithmetic  8.32 us (2%)
    psum x1, waiting for transfers between devices, shards(): lax.psum((first_grad, first_bgrad, second_grad, second_bgrad), ('smp', 'g...  142 us
    psum x1, blocking collectives, shards(): lax.psum((first_grad, first_bgrad, second_grad, second_bgrad), ('smp', 'g...  78.4 us
    ppermute x6, waiting for transfers between devices, extended(): after = lax.ppermute(initial, axis, down)  19.7 us
    ppermute x6, waiting for transfers between devices, extended(): before = lax.ppermute(last, axis, up)  16.3 us
    dot_general x18, matrix products, correlate(): jnp.einsum('soxyz,skxyz->ok', upstream, stacked, preferred_element_type=j...  12.8 us
    ppermute x6, starting transfers between devices, extended(): after = lax.ppermute(initial, axis, down)  12.4 us
    ppermute x6, starting transfers between devices, extended(): before = lax.ppermute(last, axis, up)  9.18 us
    dot_general x27, matrix products, convolve(): jnp.einsum('ok,skxyz->soxyz', tap_block, stacked, preferred_element_type=...  8.76 us
  transfers between devices with their start and end apart: 13, of which 7 were waited for; matrix products, arithmetic and copies ran while one was open for 2% of the time, Pallas kernels for 0%

commit v1 on v0

--- a/solution.py
+++ b/solution.py
@@ -101,7 +101,7 @@
     first_grad = correlate(preact_grad, input_pad) * grad_scale
     first_bgrad = jnp.sum(preact_grad, axis=(0, 2, 3, 4), dtype=jnp.float32) * grad_scale
     first_grad, first_bgrad, second_grad, second_bgrad = lax.psum(
-        (first_grad, first_bgrad, second_grad, second_bgrad), ("smp", "gx", "gz")
+        lax.psum((first_grad, first_bgrad, second_grad, second_bgrad), ("gx", "gz")), "smp"
     )
     return (output, first_grad, first_bgrad, second_grad, second_bgrad)
 

time: 337 us -> 325 us (0.964)
  blocking collectives: 78.4 us -> 65.8 us
  waiting for transfers between devices: 178 us -> 173 us
  matrix products: 21.5 us -> 25.4 us
    psum x1 -> x2, blocking collectives: 78.4 us -> 65.8 us  [the longest x1 41 us: shards(): lax.psum((first_grad, first_bgrad, second_grad, second_bgrad), ('gx', 'gz'))]
    psum x1 -> x2, waiting for transfers between devices: 142 us -> 137 us  [the longest x1 76.7 us: shards(): lax.psum((first_grad, first_bgrad, second_grad, second_bgrad), ('gx', 'gz'))]
    dot_general x27, matrix products: 8.76 us -> 12.6 us  [convolve(): jnp.einsum('ok,skxyz->soxyz', tap_block, stacked, preferred_element_type=...]
  transfers between devices with their start and end apart: 13 -> 14, of which waited for: 7 -> 8; matrix products, arithmetic and copies ran while one was open for 2% -> 4% of each run, Pallas kernels for 0% -> 0%
where the time goes in v1:
time: 325 us; the launch traced here: 323 us
  waiting for transfers between devices  173 us (53%)
  blocking collectives  65.8 us (20%)
  matrix products  25.4 us (8%)
  starting transfers between devices  21.6 us (7%)
  between operations  14.6 us (4%)
  local copies, waits for them, and re-layouts  14 us (4%)
  other arithmetic  8.32 us (3%)
    psum x1, waiting for transfers between devices, shards(): lax.psum((first_grad, first_bgrad, second_grad, second_bgrad), ('gx', 'gz'))  76.7 us
    psum x1, waiting for transfers between devices, shards(): lax.psum(lax.psum((first_grad, first_bgrad, second_grad, second_bgrad), (...  60.2 us
    psum x1, blocking collectives, shards(): lax.psum((first_grad, first_bgrad, second_grad, second_bgrad), ('gx', 'gz'))  41 us
    psum x1, blocking collectives, shards(): lax.psum(lax.psum((first_grad, first_bgrad, second_grad, second_bgrad), (...  24.8 us
    ppermute x6, waiting for transfers between devices, extended(): after = lax.ppermute(initial, axis, down)  19.7 us
    ppermute x6, waiting for transfers between devices, extended(): before = lax.ppermute(last, axis, up)  16.3 us
    dot_general x18, matrix products, correlate(): jnp.einsum('soxyz,skxyz->ok', upstream, stacked, preferred_element_type=j...  12.7 us
    dot_general x27, matrix products, convolve(): jnp.einsum('ok,skxyz->soxyz', tap_block, stacked, preferred_element_type=...  12.6 us
  transfers between devices with their start and end apart: 14, of which 8 were waited for; matrix products, arithmetic and copies ran while one was open for 4% of the time, Pallas kernels for 0%

profile of v1, /device:TPU:1, one launch (start us, length us, event | category | flops | bytes accessed | tf_op | source)
XLA Modules:
  0.0 322.7 jit_solution(10904312133715604605)
XLA Ops:
  7.2 1.1 copy.113
  8.3 4.7 %collective-permute-start.9 = (bf16[1,32,1,8,128]{4,1,3,2,0:T(8,128)(2,1)S(1)}, bf16[1,32,1,8,128]{4,1,3,2,0:T(8,128)(2,1)S(1)}, u32[]{:S(2)}, u32[]{:S(2)}) collective-permute-start(bf16[1,32,1,8,128]{4,1,3,2,0:T(8,128)(2,1)S(1)} %get-tuple-element.109), channel_id=1, source_target_pairs={{2,0},{4,2},{6,4},{8,6},{10,8},{12,10},{14,12},{0,14},{3,1},{5,3},... | collective-permute-start | bytes 196616 | tf_op jit(solution)/shard_map/ppermute | solution.py:15
  13.1 1.1 copy.88
  14.2 3.6 %collective-permute-start.1 = (bf16[1,32,1,8,128]{4,1,3,2,0:T(8,128)(2,1)S(1)}, bf16[1,32,1,8,128]{4,1,3,2,0:T(8,128)(2,1)S(1)}, u32[]{:S(2)}, u32[]{:S(2)}) collective-permute-start(bf16[1,32,1,8,128]{4,1,3,2,0:T(8,128)(2,1)S(1)} %get-tuple-element.113), channel_id=1, source_target_pairs={{2,0},{4,2},{6,4},{8,6},{10,8},{12,10},{14,12},{0,14},{3,1},{5,3},... | collective-permute-start | bytes 196616 | tf_op jit(solution)/shard_map/ppermute | solution.py:15
  20.6 2.4 collective-permute-done
  23.1 3.4 %collective-permute-start.10 = (bf16[1,32,7,8,1]{4,1,3,2,0:T(8,128)(2,1)S(1)}, bf16[1,32,7,8,1]{4,1,3,2,0:T(8,128)(2,1)S(1)}, u32[]{:S(2)}, u32[]{:S(2)}) collective-permute-start(bf16[1,32,7,8,1]{4,1,3,2,0:T(8,128)(2,1)S(1)} %get-tuple-element.93), channel_id=1, source_target_pairs={{0,1},{1,0},{2,3},{3,2},{4,5},{5,4},{6,7},{7,6},{8,9},{9,8},{10,11... | collective-permute-start | bytes 10760 | tf_op jit(solution)/shard_map/ppermute | solution.py:14
  26.8 3.0 collective-permute-start.2
  29.8 4.7 %collective-permute-done.10 = bf16[1,32,7,8,1]{4,1,3,2,0:T(8,128)(2,1)S(1)} collective-permute-done((bf16[1,32,7,8,1]{4,1,3,2,0:T(8,128)(2,1)S(1)}, bf16[1,32,7,8,1]{4,1,3,2,0:T(8,128)(2,1)S(1)}, u32[]{:S(2)}, u32[]{:S(2)}) %collective-permute-start.10) | collective-permute-done | bytes 3616 | tf_op jit(solution)/shard_map/ppermute | solution.py:14
  34.5 9.8 %collective-permute-done.11 = bf16[1,32,7,8,1]{4,1,3,2,0:T(8,128)(2,1)S(1)} collective-permute-done((bf16[1,32,7,8,1]{4,1,3,2,0:T(8,128)(2,1)S(1)}, bf16[1,32,7,8,1]{4,1,3,2,0:T(8,128)(2,1)S(1)}, u32[]{:S(2)}, u32[]{:S(2)}) %collective-permute-start.11) | collective-permute-done | bytes 3616 | tf_op jit(solution)/shard_map/ppermute | solution.py:15
  44.9 1.5 fusion.148
  46.5 7.7 %collective-permute-done.2 = bf16[1,32,7,8,1]{4,1,3,2,0:T(8,128)(2,1)S(1)} collective-permute-done((bf16[1,32,7,8,1]{4,1,3,2,0:T(8,128)(2,1)S(1)}, bf16[1,32,7,8,1]{4,1,3,2,0:T(8,128)(2,1)S(1)}, u32[]{:S(2)}, u32[]{:S(2)}) %collective-permute-start.2) | collective-permute-done | bytes 3616 | tf_op jit(solution)/shard_map/ppermute | solution.py:14
  54.2 9.8 %collective-permute-done.3 = bf16[1,32,7,8,1]{4,1,3,2,0:T(8,128)(2,1)S(1)} collective-permute-done((bf16[1,32,7,8,1]{4,1,3,2,0:T(8,128)(2,1)S(1)}, bf16[1,32,7,8,1]{4,1,3,2,0:T(8,128)(2,1)S(1)}, u32[]{:S(2)}, u32[]{:S(2)}) %collective-permute-start.3) | collective-permute-done | bytes 3616 | tf_op jit(solution)/shard_map/ppermute | solution.py:15
  64.6 1.5 fusion.150
  67.1 1.1 pad_maximum_fusion.14
  74.3 1.0 convolution_add_fusion.1
  82.5 3.6 %collective-permute-start.5 = (bf16[1,32,1,8,128]{4,1,3,2,0:T(8,128)(2,1)S(1)}, bf16[1,32,1,8,128]{4,1,3,2,0:T(8,128)(2,1)S(1)}, u32[]{:S(2)}, u32[]{:S(2)}) collective-permute-start(bf16[1,32,1,8,128]{4,1,3,2,0:T(8,128)(2,1)S(1)} %get-tuple-element.112), channel_id=1, source_target_pairs={{2,0},{4,2},{6,4},{8,6},{10,8},{12,10},{14,12},{0,14},{3,1},{5,3},... | collective-permute-start | bytes 196616 | tf_op jit(solution)/shard_map/ppermute | solution.py:15
  86.1 1.6 collective-permute-done.4
  88.0 2.8 collective-permute-start.6
  91.0 0.8 maximum_multiply_fusion
  91.8 41.0 %all-reduce.3 = (f32[32]{0:T(128)S(1)}, f32[32]{0:T(128)S(1)}) all-reduce(f32[32]{0:T(128)S(1)} %broadcast_multiply_fusion.1, f32[32]{0:T(128)S(1)} %broadcast_multiply_fusion), channel_id=1, replica_groups=mesh['smp'=8,'gx'=8,'gz'=2] {'gx','gz'}, use_global_device_ids=true, to_apply=%region_3.4 | all-reduce | flops 64 | bytes 512 | tf_op jit(solution)/shard_map/psum | solution.py:104
  132.8 24.8 %all-reduce.5 = (f32[32]{0:T(128)}, f32[32]{0:T(128)}) all-reduce(f32[32]{0:T(128)S(1)} %get-tuple-element.15, f32[32]{0:T(128)S(1)} %get-tuple-element.16), channel_id=1, replica_groups=mesh['smp'=8,'gx'=8,'gz'=2] {'smp'}, use_global_device_ids=true, to_apply=%region_4.5 | all-reduce | flops 64 | bytes 512 | tf_op jit(solution)/shard_map/psum | solution.py:103
  160.5 0.7 convolution_bitcast_fusion.16
  161.8 1.4 fusion.149
  169.7 1.1 convolution_add_fusion.10
  170.9 0.8 maximum_multiply_fusion.1
  171.8 2.2 convolution_add_fusion.9
  174.0 76.7 %all-reduce.10.cloned.1.call-done = (f32[32,3,3,3,32]{4,0,3,2,1:T(8,128)}, f32[32,3,3,3,32]{4,0,3,2,1:T(8,128)}) async-done(((f32[32,3,3,3,32]{4,0,3,2,1:T(8,128)}, f32[32,3,3,3,32]{4,0,3,2,1:T(8,128)}), (f32[32,3,3,3,32]{4,0,3,2,1:T(8,128)}, f32[32,3,3,3,32]{4,0,3,2,1:T(8,128)})) %all-reduce.10.cloned.1.call-update) | async-done | bytes 221200 | tf_op jit(solution)/shard_map/psum | solution.py:104
  250.8 1.4 fusion.12
  252.2 0.9 copy.164
  253.0 60.2 %all-reduce.12.cloned.1.call-done = (f32[32,3,3,3,32]{4,0,3,2,1:T(8,128)}, f32[32,3,3,3,32]{4,0,3,2,1:T(8,128)}) async-done(((f32[32,3,3,3,32]{4,0,3,2,1:T(8,128)}, f32[32,3,3,3,32]{4,0,3,2,1:T(8,128)}), (f32[32,3,3,3,32]{4,0,3,2,1:T(8,128)}, f32[32,3,3,3,32]{4,0,3,2,1:T(8,128)})) %all-reduce.12.cloned.1.call-update) | async-done | bytes 221200 | tf_op jit(solution)/shard_map/psum | solution.py:103
  313.2 1.9 copy.330
  315.1 0.8 copy.331
  (146 shorter events, 29.0 us)
Async XLA Ops:
  7.2 10.6 %copy-start = (bf16[1,32,5,8,128]{4,3,2,1,0:T(8,128)(2,1)S(1)}, bf16[1,32,5,8,128]{4,3,2,1,0:T(8,128)(2,1)}, u32[]{:S(2)}) copy-start(bf16[1,32,5,8,128]{4,3,2,1,0:T(8,128)(2,1)} %param.11) | copy-start | bytes 983044
  7.2 10.9 %copy-start.2 = (bf16[32,3,3,3,32]{4,0,3,2,1:T(8,128)(2,1)S(1)}, bf16[32,3,3,3,32]{4,0,3,2,1:T(8,128)(2,1)}, u32[]{:S(2)}) copy-start(bf16[32,3,3,3,32]{4,0,3,2,1:T(8,128)(2,1)} %param.9) | copy-start | bytes 165892
  7.2 243.6 %all-reduce.10.cloned.1.call-start = ((), (), s32[]{:S(2)}) async-start(), calls=%async_computation | async-start | bytes 1769472 | tf_op jit(solution)/shard_map/psum | solution.py:104
  8.3 12.0 %collective-permute-start.9 = (bf16[1,32,1,8,128]{4,1,3,2,0:T(8,128)(2,1)S(1)}, bf16[1,32,1,8,128]{4,1,3,2,0:T(8,128)(2,1)S(1)}, u32[]{:S(2)}, u32[]{:S(2)}) collective-permute-start(bf16[1,32,1,8,128]{4,1,3,2,0:T(8,128)(2,1)S(1)} %get-tuple-element.109), channel_id=1, source_target_pairs={{2,0},{4,2},{6,4},{8,6},{10,8},{12,10},{14,12},{0,14},{3,1},{5,3},... | collective-permute-start | bytes 196616 | tf_op jit(solution)/shard_map/ppermute | solution.py:15
  13.1 5.1 %copy-start.4 = (bf16[32,3,3,3,32]{4,0,3,2,1:T(8,128)(2,1)S(1)}, bf16[32,3,3,3,32]{4,0,3,2,1:T(8,128)(2,1)}, u32[]{:S(2)}) copy-start(bf16[32,3,3,3,32]{4,0,3,2,1:T(8,128)(2,1)} %param.7) | copy-start | bytes 165892
  13.1 7.2 %collective-permute-start.8 = (bf16[1,32,1,8,128]{4,1,3,2,0:T(8,128)(2,1)S(1)}, bf16[1,32,1,8,128]{4,1,3,2,0:T(8,128)(2,1)S(1)}, u32[]{:S(2)}, u32[]{:S(2)}) collective-permute-start(bf16[1,32,1,8,128]{4,1,3,2,0:T(8,128)(2,1)S(1)} %get-tuple-element.110), channel_id=1, source_target_pairs={{0,2},{2,4},{4,6},{6,8},{8,10},{10,12},{12,14},{14,0},{1,3},{3,5},... | collective-permute-start | bytes 196616 | tf_op jit(solution)/shard_map/ppermute | solution.py:14
  14.2 12.4 %collective-permute-start.1 = (bf16[1,32,1,8,128]{4,1,3,2,0:T(8,128)(2,1)S(1)}, bf16[1,32,1,8,128]{4,1,3,2,0:T(8,128)(2,1)S(1)}, u32[]{:S(2)}, u32[]{:S(2)}) collective-permute-start(bf16[1,32,1,8,128]{4,1,3,2,0:T(8,128)(2,1)S(1)} %get-tuple-element.113), channel_id=1, source_target_pairs={{2,0},{4,2},{6,4},{8,6},{10,8},{12,10},{14,12},{0,14},{3,1},{5,3},... | collective-permute-start | bytes 196616 | tf_op jit(solution)/shard_map/ppermute | solution.py:15
  17.8 5.2 %collective-permute-start = (bf16[1,32,1,8,128]{4,1,3,2,0:T(8,128)(2,1)S(1)}, bf16[1,32,1,8,128]{4,1,3,2,0:T(8,128)(2,1)S(1)}, u32[]{:S(2)}, u32[]{:S(2)}) collective-permute-start(bf16[1,32,1,8,128]{4,1,3,2,0:T(8,128)(2,1)S(1)} %get-tuple-element.114), channel_id=1, source_target_pairs={{0,2},{2,4},{4,6},{6,8},{8,10},{10,12},{12,14},{14,0},{1,3},{3,5},... | collective-permute-start | bytes 196616 | tf_op jit(solution)/shard_map/ppermute | solution.py:14
  20.3 2.7 copy-start.1
  23.1 11.4 %collective-permute-start.10 = (bf16[1,32,7,8,1]{4,1,3,2,0:T(8,128)(2,1)S(1)}, bf16[1,32,7,8,1]{4,1,3,2,0:T(8,128)(2,1)S(1)}, u32[]{:S(2)}, u32[]{:S(2)}) collective-permute-start(bf16[1,32,7,8,1]{4,1,3,2,0:T(8,128)(2,1)S(1)} %get-tuple-element.93), channel_id=1, source_target_pairs={{0,1},{1,0},{2,3},{3,2},{4,5},{5,4},{6,7},{7,6},{8,9},{9,8},{10,11... | collective-permute-start | bytes 10760 | tf_op jit(solution)/shard_map/ppermute | solution.py:14
  26.5 17.9 %collective-permute-start.11 = (bf16[1,32,7,8,1]{4,1,3,2,0:T(8,128)(2,1)S(1)}, bf16[1,32,7,8,1]{4,1,3,2,0:T(8,128)(2,1)S(1)}, u32[]{:S(2)}, u32[]{:S(2)}) collective-permute-start(bf16[1,32,7,8,1]{4,1,3,2,0:T(8,128)(2,1)S(1)} %get-tuple-element.94), channel_id=1, source_target_pairs={{1,0},{0,1},{3,2},{2,3},{5,4},{4,5},{7,6},{6,7},{9,8},{8,9},{11,10... | collective-permute-start | bytes 10760 | tf_op jit(solution)/shard_map/ppermute | solution.py:15
  26.8 27.4 %collective-permute-start.2 = (bf16[1,32,7,8,1]{4,1,3,2,0:T(8,128)(2,1)S(1)}, bf16[1,32,7,8,1]{4,1,3,2,0:T(8,128)(2,1)S(1)}, u32[]{:S(2)}, u32[]{:S(2)}) collective-permute-start(bf16[1,32,7,8,1]{4,1,3,2,0:T(8,128)(2,1)S(1)} %get-tuple-element.101), channel_id=1, source_target_pairs={{0,1},{1,0},{2,3},{3,2},{4,5},{5,4},{6,7},{7,6},{8,9},{9,8},{10,11... | collective-permute-start | bytes 10760 | tf_op jit(solution)/shard_map/ppermute | solution.py:14
  29.8 34.3 %collective-permute-start.3 = (bf16[1,32,7,8,1]{4,1,3,2,0:T(8,128)(2,1)S(1)}, bf16[1,32,7,8,1]{4,1,3,2,0:T(8,128)(2,1)S(1)}, u32[]{:S(2)}, u32[]{:S(2)}) collective-permute-start(bf16[1,32,7,8,1]{4,1,3,2,0:T(8,128)(2,1)S(1)} %get-tuple-element.102), channel_id=1, source_target_pairs={{1,0},{0,1},{3,2},{2,3},{5,4},{4,5},{7,6},{6,7},{9,8},{8,9},{11,10... | collective-permute-start | bytes 10760 | tf_op jit(solution)/shard_map/ppermute | solution.py:15
  70.5 0.7 copy-start.5
  82.4 5.3 %collective-permute-start.4 = (bf16[1,32,1,8,128]{4,1,3,2,0:T(8,128)(2,1)S(1)}, bf16[1,32,1,8,128]{4,1,3,2,0:T(8,128)(2,1)S(1)}, u32[]{:S(2)}, u32[]{:S(2)}) collective-permute-start(bf16[1,32,1,8,128]{4,1,3,2,0:T(8,128)(2,1)S(1)} %get-tuple-element.111), channel_id=1, source_target_pairs={{0,2},{2,4},{4,6},{6,8},{8,10},{10,12},{12,14},{14,0},{1,3},{3,5},... | collective-permute-start | bytes 196616 | tf_op jit(solution)/shard_map/ppermute | solution.py:14
  82.5 5.2 %collective-permute-start.5 = (bf16[1,32,1,8,128]{4,1,3,2,0:T(8,128)(2,1)S(1)}, bf16[1,32,1,8,128]{4,1,3,2,0:T(8,128)(2,1)S(1)}, u32[]{:S(2)}, u32[]{:S(2)}) collective-permute-start(bf16[1,32,1,8,128]{4,1,3,2,0:T(8,128)(2,1)S(1)} %get-tuple-element.112), channel_id=1, source_target_pairs={{2,0},{4,2},{6,4},{8,6},{10,8},{12,10},{14,12},{0,14},{3,1},{5,3},... | collective-permute-start | bytes 196616 | tf_op jit(solution)/shard_map/ppermute | solution.py:15
  88.0 69.7 %collective-permute-start.6 = (bf16[1,32,7,8,1]{4,1,3,2,0:T(8,128)(2,1)S(1)}, bf16[1,32,7,8,1]{4,1,3,2,0:T(8,128)(2,1)S(1)}, u32[]{:S(2)}, u32[]{:S(2)}) collective-permute-start(bf16[1,32,7,8,1]{4,1,3,2,0:T(8,128)(2,1)S(1)} %get-tuple-element.97), channel_id=1, source_target_pairs={{0,1},{1,0},{2,3},{3,2},{4,5},{5,4},{6,7},{7,6},{8,9},{9,8},{10,11... | collective-permute-start | bytes 10760 | tf_op jit(solution)/shard_map/ppermute | solution.py:14
  90.7 66.9 %collective-permute-start.7 = (bf16[1,32,7,8,1]{4,1,3,2,0:T(8,128)(2,1)S(1)}, bf16[1,32,7,8,1]{4,1,3,2,0:T(8,128)(2,1)S(1)}, u32[]{:S(2)}, u32[]{:S(2)}) collective-permute-start(bf16[1,32,7,8,1]{4,1,3,2,0:T(8,128)(2,1)S(1)} %get-tuple-element.98), channel_id=1, source_target_pairs={{1,0},{0,1},{3,2},{2,3},{5,4},{4,5},{7,6},{6,7},{9,8},{8,9},{11,10... | collective-permute-start | bytes 10760 | tf_op jit(solution)/shard_map/ppermute | solution.py:15
  171.8 79.0 %copy-start.6 = (f32[32]{0:T(128)S(1)}, f32[32]{0:T(128)}, u32[]{:S(2)}) copy-start(f32[32]{0:T(128)} %param.10) | copy-start | bytes 388
  171.8 141.5 %all-reduce.12.cloned.1.call-start = ((), (), s32[]{:S(2)}) async-start(), calls=%async_computation.1 | async-start | bytes 1769472 | tf_op jit(solution)/shard_map/psum | solution.py:103
  313.2 1.9 copy-start.3
Sparse Core Ops, SparseCore 0:
  171.9 78.8 all-reduce.9
  253.3 59.9 all-reduce.11
